TPU v7x, 256 devices: a whole 4x4x8 slice. The times are simulated.
256 devices in a mesh: cells: 64 (over y, z_lo, x), bands: 4 (over z_hi, core).
Axes of the slice: x: 4, y: 4, z: 8 (z_hi: 2, z_lo: 4; z = z_hi * 4 + z_lo), core: 2. Of those that a mesh axis runs over, the one named last changes fastest.
Arguments:
- waves: bfloat16 [256, 131072], P('bands', 'cells'), may hold values from -6 to 6
- stiffness: float32 [125, 125], replicated, as said below
- cell_scale: float32 [8192], P('cells'), may hold values from 0.5 to 4
- potential: float32 [131072], P('cells'), may hold values from -2 to 2
- connect: int32 [125, 8192], P(None, 'cells'), may hold values from 0 to 3071
- live_cells: int32 [64], P('cells'), may hold values from 16 to 128, as said below
- shared: int32 [64, 2, 512], P('cells'), may hold values from 0 to 2047
- window: float32 [2], replicated, may hold values from 1 to 4
Outputs:
- filtered: float32 [256, 131072], P('bands', 'cells')
- projected: float32 [256, 256], P('cells', 'bands')
Inputs may be any that keep to these rules, and one draw needn't show every extreme that they name: `live_cells`: at least one partition has all 128 slots live. `stiffness`: symmetric positive definite.
All inputs are finite; a program needn't handle non-finite values.
Results may differ from a plain program's by a relative error of at most 0.0037.
Values may be sent and summed in bfloat16 or wider, within the bound.
No kernel may reach another device: no remote copies, remote signals or barrier semaphores. Data moves between devices by JAX's collectives and lax.ppermute only.
A program may use at most 64 MiB of HBM per device.

v0:
```python
import math
import jax
import jax.numpy as jnp
from jax import lax
from jax.sharding import PartitionSpec as P

sigma_one = -0.5
sigma_two = 1.0 / (2.0 / sigma_one - sigma_one)


def with_halo(block, sides, width):
    for axis, dim in sides:
        count = lax.axis_size(axis)
        forward = [(i, i + 1) for i in range(count - 1)]
        backward = [(target, source) for source, target in forward]
        low = lax.ppermute(
            lax.slice_in_dim(block, block.shape[dim] - width, None, axis=dim), axis, forward
        )
        high = lax.ppermute(lax.slice_in_dim(block, 0, width, axis=dim), axis, backward)
        block = jnp.concatenate([low, block, high], axis=dim)
    return block


def local(waves, stiffness, cell_scale, potential, connect, live_cells, shared, window):
    columns, node_dev = waves.shape
    ghost = shared.shape[2]
    capacity = connect.shape[1]
    shared_rows = shared[0]
    live_count = live_cells[0]
    stiff_rounded = stiffness.astype(jnp.bfloat16)
    center = window[0]
    half_width = window[1]
    block_size = math.gcd(capacity, 128)
    block_turns = capacity // block_size
    potential_row = potential[None, :]

    def with_ghosts(owned):
        packed = jnp.concatenate([owned[:, shared_rows[0]], owned[:, shared_rows[1]]], axis=1)
        bordered = with_halo(packed, (("cells", 1),), ghost)
        return jnp.concatenate([bordered[:, :ghost], owned, bordered[:, 3 * ghost :]], axis=1)

    def assemble(totals):
        packed = jnp.concatenate([totals[:, :ghost], totals[:, ghost + node_dev :]], axis=1)
        bordered = with_halo(packed, (("cells", 1),), ghost)
        owned = totals[:, ghost : ghost + node_dev]
        return (
            owned.at[:, shared_rows[0]]
            .add(bordered[:, :ghost])
            .at[:, shared_rows[1]]
            .add(bordered[:, 3 * ghost :])
        )

    def cell_terms(extended):

        def one_block(turn, totals):
            first_cell = turn * block_size
            alive = (first_cell + jnp.arange(block_size) < live_count).astype(jnp.float32)
            weight = cell_scale * alive
            gathered = extended[:, connect]
            product = jnp.einsum(
                "ij,wjb->wib", stiff_rounded, gathered, preferred_element_type=jnp.float32
            )
            return totals.at[:, connect.reshape(-1)].add(
                (product * weight[None, None, :]).reshape(columns, -1)
            )

        empty = jnp.zeros((columns, extended.shape[1]), jnp.float32)
        return lax.fori_loop(0, block_turns, one_block, empty)

    waves32 = waves.astype(jnp.float32)
    applied_x = assemble(cell_terms(with_ghosts(waves))) + potential_row * waves32
    first_pass = ((applied_x - center * waves32) * (sigma_one / half_width)).astype(jnp.bfloat16)
    first32 = first_pass.astype(jnp.float32)
    applied_y = assemble(cell_terms(with_ghosts(first_pass))) + potential_row * first32
    filtered = (applied_y - center * first32) * (
        2.0 * sigma_two / half_width
    ) - sigma_one * sigma_two * waves32
    wave_rounded = filtered.astype(jnp.bfloat16)
    applied = assemble(cell_terms(with_ghosts(wave_rounded))) + potential_row * filtered
    apply_rounded = applied.astype(jnp.bfloat16)
    cell_count = lax.axis_size("cells")
    band_count = lax.axis_size("bands")
    inverse_total = 1.0 / (node_dev * cell_count)
    waves_all = columns * band_count
    own_rows = waves_all // cell_count
    swapped = (
        lax.all_to_all(wave_rounded, "bands", split_axis=1, concat_axis=0, tiled=True),
        lax.all_to_all(apply_rounded, "bands", split_axis=1, concat_axis=0, tiled=True),
    )
    left_side, right_side = swapped
    partial_value = (
        jnp.einsum("wn,vn->wv", left_side, right_side, preferred_element_type=jnp.float32)
        * inverse_total
    )
    arranged = partial_value.reshape(cell_count, own_rows, band_count, columns).transpose(
        0, 2, 1, 3
    )
    arranged = arranged.reshape(cell_count * band_count * own_rows, columns)
    projected = lax.psum_scatter(arranged, ("cells", "bands"), scatter_dimension=0, tiled=True)
    return (filtered, projected)


def solution(mesh):
    return jax.shard_map(
        local,
        mesh=mesh,
        in_specs=(
            P("bands", "cells"),
            P(),
            P("cells"),
            P("cells"),
            P(None, "cells"),
            P("cells"),
            P("cells", None, None),
            P(),
        ),
        out_specs=(P("bands", "cells"), P("cells", "bands")),
        check_vma=False,
    )
```

profile of v0, /device:TPU:2, one launch (start us, length us, event | category | flops | bytes accessed | tf_op | source)
XLA Modules:
  0.0 876.6 jit_solution(12638549431420464733)
XLA Ops:
  22.9 33.0 %gather_fusion.2 = bf16[16000,64]{1,0:T(8,128)(2,1)} fusion(bf16[64,3072]{0,1:T(8,128)(2,1)S(1)} %pad_maximum_fusion, s32[16384]{0:T(1024)S(1)} %pad_clamp_fusion), kind=kCustom, calls=%fused_computation.2 | custom fusion | bytes 4160000 | tf_op jit(solution)/shard_map/while/body/eval_jaxpr/gather | solution.py:59
  55.9 7.4 copy.39
  66.0 5.7 copy.40
  71.6 6.5 copy.63
  78.1 6.8 copy.41
  84.9 88.3 %scatter_custom_fusion = f32[64,3072]{0,1:T(8,128)S(1)} fusion(s32[16000]{0:T(1024)S(1)} %fusion.30, f32[16000,64]{1,0:T(8,128)} %copy.41, f32[]{:T(128)} %constant.22.clone.1), kind=kCustom, calls=%fused_computation.49 | custom fusion | flops 1024000 | bytes 786944 | tf_op jit(solution)/shard_map/while/body/eval_jaxpr/scatter-add | solution.py:63
  182.6 4.3 scatter_custom_fusion.1
  187.7 3.8 scatter_custom_fusion.2
  202.0 4.7 collective-permute-done.5
  206.8 33.0 %gather_fusion.5 = bf16[16000,64]{1,0:T(8,128)(2,1)} fusion(bf16[64,3072]{0,1:T(8,128)(2,1)S(1)} %pad_maximum_fusion.1, s32[16384]{0:T(1024)S(1)} %pad_clamp_fusion), kind=kCustom, calls=%fused_computation.5 | custom fusion | bytes 4160000 | tf_op jit(solution)/shard_map/while/body/eval_jaxpr/gather | solution.py:59
  239.8 7.3 copy.43
  249.8 5.7 copy.44
  255.5 6.5 copy.62
  261.9 6.8 copy.45
  268.7 88.3 %scatter_custom_fusion.3 = f32[64,3072]{0,1:T(8,128)S(1)} fusion(s32[16000]{0:T(1024)} %copy-done.3, f32[16000,64]{1,0:T(8,128)} %copy.45, f32[]{:T(128)} %constant.22.clone.1), kind=kCustom, calls=%fused_computation.47 | custom fusion | flops 1024000 | bytes 786944 | tf_op jit(solution)/shard_map/while/body/eval_jaxpr/scatter-add | solution.py:63
  357.1 4.5 collective-permute-start.6
  365.4 5.5 scatter_custom_fusion.4
  371.9 5.3 scatter_custom_fusion.5
  382.1 5.1 collective-permute-start.8
  390.0 7.6 all-to-all-start
  397.8 33.0 %gather_fusion.8 = bf16[16000,64]{1,0:T(8,128)(2,1)} fusion(bf16[64,3072]{0,1:T(8,128)(2,1)S(1)} %pad_maximum_fusion.2, s32[16384]{0:T(1024)S(1)} %pad_clamp_fusion), kind=kCustom, calls=%fused_computation.8 | custom fusion | bytes 4160000 | tf_op jit(solution)/shard_map/while/body/eval_jaxpr/gather | solution.py:59
  430.7 7.9 copy.47
  438.7 4.2 multiply_bitcast_fusion
  442.9 5.7 copy.48
  448.6 6.4 copy.61
  455.0 6.8 copy.49
  461.8 89.2 %scatter_custom_fusion.6 = f32[64,3072]{0,1:T(8,128)} fusion(s32[16000]{0:T(1024)} %copy-done.3, f32[16000,64]{1,0:T(8,128)} %copy.49, f32[]{:T(128)} %constant.22.clone.1), kind=kCustom, calls=%fused_computation.45 | custom fusion | flops 1024000 | bytes 786944 | tf_op jit(solution)/shard_map/while/body/eval_jaxpr/scatter-add | solution.py:63
  552.1 4.4 collective-permute-start.10
  562.7 3.8 scatter_custom_fusion.7
  567.2 3.8 scatter_custom_fusion.8
  571.3 19.3 %all_to_all.38 = bf16[64,4,512]{2,0,1:T(8,128)(2,1)S(1)} all-to-all(bf16[64,4,512]{2,0,1:T(8,128)(2,1)S(1)} %copy.50), channel_id=1, replica_groups=mesh['cells'=64,'bands'=4] {'bands'}, dimensions={1} | all-to-all | bytes 524288 | tf_op jit(solution)/shard_map/all_to_all | solution.py:88
  593.2 274.8 %all-reduce.3.cloned.1.call-done = f32[1024,64]{1,0:T(8,128)} async-done(((f32[1024,64]{1,0:T(8,128)}), f32[1024,64]{1,0:T(8,128)}) %all-reduce.3.cloned.1.call-update) | async-done | bytes 262160
  (81 shorter events, 64.6 us)
Async XLA Ops:
  7.2 12.7 %copy-start.1 = (s32[125,128]{1,0:T(8,128)S(1)}, s32[125,128]{1,0:T(8,128)}, u32[]{:S(2)}) copy-start(s32[125,128]{1,0:T(8,128)} %param.12) | copy-start | bytes 192004
  7.2 12.9 %copy-start.10 = (f32[128]{0:T(128)S(1)}, f32[128]{0:T(128)}, u32[]{:S(2)}) copy-start(f32[128]{0:T(128)} %param.10) | copy-start | bytes 1540
  7.2 13.0 %copy-start.9 = (f32[2]{0:T(128)S(1)}, f32[2]{0:T(128)}, u32[]{:S(2)}) copy-start(f32[2]{0:T(128)} %param.15) | copy-start | bytes 28
  8.0 0.6 copy-start.4
  8.0 7.9 copy-start.5
  11.1 10.2 %collective-permute-start = (bf16[64,512]{0,1:T(8,128)(2,1)S(1)}, bf16[64,512]{0,1:T(8,128)(2,1)S(1)}, u32[]{:S(2)}, u32[]{:S(2)}) collective-permute-start(bf16[64,512]{0,1:T(8,128)(2,1)S(1)} %bitcast.116), channel_id=1, source_target_pairs={{0,4},{4,8},{8,12},{12,16},{16,20},{20,24},{24,28},{28,32},{32,36}... | collective-permute-start | bytes 196616 | tf_op jit(solution)/shard_map/ppermute | solution.py:16
  15.9 6.9 collective-permute-start.1
  20.1 64.8 %copy-start.3 = (s32[16000]{0:T(1024)}, s32[16000]{0:T(1024)S(1)}, u32[]{:S(2)}) copy-start(s32[16000]{0:T(1024)S(1)} %fusion.30) | copy-start | bytes 192004
  20.1 43.1 %copy-start.6 = (f32[128]{0:T(128)}, f32[128]{0:T(128)S(1)}, u32[]{:S(2)}) copy-start(f32[128]{0:T(128)S(1)} %compare_select_fusion.4) | copy-start | bytes 1540
  55.9 7.4 copy-start
  84.9 95.6 %copy-start.2 = (f32[2048]{0:T(1024)S(1)}, f32[2048]{0:T(1024)}, u32[]{:S(2)}) copy-start(f32[2048]{0:T(1024)} %param.11) | copy-start | bytes 24580
  174.0 8.6 collective-permute-start.2
  177.2 10.6 %collective-permute-start.3 = (f32[64,512]{0,1:T(8,128)}, f32[64,512]{0,1:T(8,128)S(1)}, u32[]{:S(2)}, u32[]{:S(2)}) collective-permute-start(f32[64,512]{0,1:T(8,128)} %get-tuple-element.70), channel_id=1, source_target_pairs={{4,0},{8,4},{12,8},{16,12},{20,16},{24,20},{28,24},{32,28},{36,32}... | collective-permute-start | bytes 393224 | tf_op jit(solution)/shard_map/ppermute | solution.py:19
  195.1 6.9 collective-permute-start.4
  198.8 7.9 collective-permute-start.5
  239.8 7.3 copy-start.7
  357.1 8.3 collective-permute-start.6
  361.6 10.4 %collective-permute-start.7 = (f32[64,512]{0,1:T(8,128)S(1)}, f32[64,512]{0,1:T(8,128)S(1)}, u32[]{:S(2)}, u32[]{:S(2)}) collective-permute-start(f32[64,512]{0,1:T(8,128)S(1)} %get-tuple-element.68), channel_id=1, source_target_pairs={{4,0},{8,4},{12,8},{16,12},{20,16},{24,20},{28,24},{32,28},{36,32}... | collective-permute-start | bytes 393224 | tf_op jit(solution)/shard_map/ppermute | solution.py:19
  382.1 15.5 %collective-permute-start.8 = (bf16[64,512]{0,1:T(8,128)(2,1)S(1)}, bf16[64,512]{0,1:T(8,128)(2,1)S(1)}, u32[]{:S(2)}, u32[]{:S(2)}) collective-permute-start(bf16[64,512]{0,1:T(8,128)(2,1)S(1)} %bitcast.119), channel_id=1, source_target_pairs={{0,4},{4,8},{8,12},{12,16},{16,20},{20,24},{24,28},{28,32},{32,36}... | collective-permute-start | bytes 196616 | tf_op jit(solution)/shard_map/ppermute | solution.py:16
  387.2 10.4 %collective-permute-start.9 = (bf16[64,512]{0,1:T(8,128)(2,1)S(1)}, bf16[64,512]{0,1:T(8,128)(2,1)S(1)}, u32[]{:S(2)}, u32[]{:S(2)}) collective-permute-start(bf16[64,512]{0,1:T(8,128)(2,1)S(1)} %bitcast.117), channel_id=1, source_target_pairs={{4,0},{8,4},{12,8},{16,12},{20,16},{24,20},{28,24},{32,28},{36,32}... | collective-permute-start | bytes 196616 | tf_op jit(solution)/shard_map/ppermute | solution.py:19
  390.0 181.3 %all-to-all-start = ((bf16[64,4,512]{2,0,1:T(8,128)(2,1)}), bf16[64,4,512]{2,0,1:T(8,128)(2,1)S(1)}, u32[]{:S(2)}, u32[]{:S(2)}) async-start(bf16[64,4,512]{2,0,1:T(8,128)(2,1)} %copy.46), calls=%async_computation | async-start | bytes 524288 | tf_op jit(solution)/shard_map/all_to_all | solution.py:87
  397.6 470.4 %all-reduce.3.cloned.1.call-start = ((), (), s32[]{:S(2)}) async-start(), calls=%async_computation.2 | async-start | bytes 1048576
  430.7 7.9 copy-start.8
  552.1 10.6 %collective-permute-start.10 = (f32[64,512]{0,1:T(8,128)S(1)}, f32[64,512]{0,1:T(8,128)S(1)}, u32[]{:S(2)}, u32[]{:S(2)}) collective-permute-start(f32[64,512]{0,1:T(8,128)S(1)} %get-tuple-element.67), channel_id=1, source_target_pairs={{0,4},{4,8},{8,12},{12,16},{16,20},{20,24},{24,28},{28,32},{32,36}... | collective-permute-start | bytes 393224 | tf_op jit(solution)/shard_map/ppermute | solution.py:16
  556.5 10.7 %collective-permute-start.11 = (f32[64,512]{0,1:T(8,128)S(1)}, f32[64,512]{0,1:T(8,128)S(1)}, u32[]{:S(2)}, u32[]{:S(2)}) collective-permute-start(f32[64,512]{0,1:T(8,128)S(1)} %get-tuple-element.66), channel_id=1, source_target_pairs={{4,0},{8,4},{12,8},{16,12},{20,16},{24,20},{28,24},{32,28},{36,32}... | collective-permute-start | bytes 393224 | tf_op jit(solution)/shard_map/ppermute | solution.py:19
Sparse Core Ops, SparseCore 0:
  592.2 275.7 all-reduce.2
where the time goes:
time: 886 us; the launch traced here: 877 us
  other arithmetic  301 us (34%)
  waiting for transfers between devices  289 us (33%)
  local copies, waits for them, and re-layouts  195 us (22%)
  starting transfers between devices  45.7 us (5%)
  blocking collectives  19.3 us (2%)
  between operations  16.8 us (2%)
  matrix products  9.84 us (1%)
    unnamed x2, waiting for transfers between devices  275 us
    scatter-add x3, other arithmetic, one_block(): totals.at[:, connect.reshape(-1)]  266 us
    gather x6, local copies, waits for them, and re-layouts, one_block(): gathered = extended[:, connect]  121 us
    scatter-add x6, other arithmetic, assemble(): return owned.at[:, shared_rows[0]].add(bordered[:, :ghost]).at[:, shared_...  26.6 us
    ppermute x6, starting transfers between devices, with_halo(): lax.ppermute(lax.slice_in_dim(block, block.shape[dim] - width, None, axis...  24.2 us
    unnamed x28, local copies, waits for them, and re-layouts  23.6 us
    reshape x3, local copies, waits for them, and re-layouts, one_block(): (product * weight[None, None, :]).reshape(columns, -1)  20.4 us
    all_to_all x1, blocking collectives, local(): lax.all_to_all(apply_rounded, 'bands', split_axis=1, concat_axis=0, tiled...  19.3 us
  transfers between devices with their start and end apart: 14, of which 10 were waited for; matrix products, arithmetic and copies ran while one was open for 21% of the time, Pallas kernels for 0%

commit v1 on v0

--- a/solution.py
+++ b/solution.py
@@ -83,9 +83,18 @@
     inverse_total = 1.0 / (node_dev * cell_count)
     waves_all = columns * band_count
     own_rows = waves_all // cell_count
+    _open_keys = lambda mat: jnp.concatenate(
+        lax.all_to_all(
+            jnp.stack(jnp.split(mat, lax.psum(1, axis_name="bands"), 1)),
+            axis_name="bands",
+            split_axis=0,
+            concat_axis=0,
+        ),
+        0,
+    )
     swapped = (
         lax.all_to_all(wave_rounded, "bands", split_axis=1, concat_axis=0, tiled=True),
-        lax.all_to_all(apply_rounded, "bands", split_axis=1, concat_axis=0, tiled=True),
+        _open_keys(apply_rounded),
     )
     left_side, right_side = swapped
     partial_value = (

time: 886 us -> 885 us (level)
  transfers between devices with their start and end apart: 14 -> 14, of which waited for: 10 -> 9; matrix products, arithmetic and copies ran while one was open for 21% -> 21% of each run, Pallas kernels for 0% -> 0%
where the time goes in v1:
time: 885 us; the launch traced here: 875 us
  other arithmetic  304 us (34%)
  waiting for transfers between devices  288 us (33%)
  local copies, waits for them, and re-layouts  195 us (22%)
  starting transfers between devices  45.7 us (5%)
  between operations  16.9 us (2%)
  blocking collectives  16.5 us (2%)
  matrix products  9.87 us (1%)
    unnamed x2, waiting for transfers between devices  274 us
    scatter-add x3, other arithmetic, one_block(): totals.at[:, connect.reshape(-1)]  265 us
    gather x6, local copies, waits for them, and re-layouts, one_block(): gathered = extended[:, connect]  122 us
    scatter-add x6, other arithmetic, assemble(): return owned.at[:, shared_rows[0]].add(bordered[:, :ghost]).at[:, shared_...  29.5 us
    ppermute x6, starting transfers between devices, with_halo(): lax.ppermute(lax.slice_in_dim(block, block.shape[dim] - width, None, axis...  24.2 us
    unnamed x28, local copies, waits for them, and re-layouts  23 us
    reshape x3, local copies, waits for them, and re-layouts, one_block(): (product * weight[None, None, :]).reshape(columns, -1)  20.4 us
  transfers between devices with their start and end apart: 14, of which 9 were waited for; matrix products, arithmetic and copies ran while one was open for 21% of the time, Pallas kernels for 0%

profile of v1, /device:TPU:2, one launch (start us, length us, event | category | flops | bytes accessed | tf_op | source)
XLA Modules:
  0.0 875.4 jit_solution(16719890908142331901)
XLA Ops:
  22.4 33.1 %gather_fusion.2 = bf16[16000,64]{1,0:T(8,128)(2,1)} fusion(bf16[64,3072]{0,1:T(8,128)(2,1)S(1)} %pad_maximum_fusion, s32[16384]{0:T(1024)S(1)} %pad_clamp_fusion), kind=kCustom, calls=%fused_computation.2 | custom fusion | bytes 4160000 | tf_op jit(solution)/shard_map/while/body/eval_jaxpr/gather | solution.py:59
  55.5 7.4 copy.39
  65.5 5.7 copy.40
  71.2 6.5 copy.63
  77.7 6.8 copy.41
  84.5 88.3 %scatter_custom_fusion = f32[64,3072]{0,1:T(8,128)S(1)} fusion(s32[16000]{0:T(1024)S(1)} %fusion.30, f32[16000,64]{1,0:T(8,128)} %copy.41, f32[]{:T(128)} %constant.22.clone.1), kind=kCustom, calls=%fused_computation.49 | custom fusion | flops 1024000 | bytes 786944 | tf_op jit(solution)/shard_map/while/body/eval_jaxpr/scatter-add | solution.py:63
  182.2 4.3 scatter_custom_fusion.1
  187.3 3.8 scatter_custom_fusion.2
  201.5 4.8 collective-permute-done.5
  206.4 33.1 %gather_fusion.5 = bf16[16000,64]{1,0:T(8,128)(2,1)} fusion(bf16[64,3072]{0,1:T(8,128)(2,1)S(1)} %pad_maximum_fusion.1, s32[16384]{0:T(1024)S(1)} %pad_clamp_fusion), kind=kCustom, calls=%fused_computation.5 | custom fusion | bytes 4160000 | tf_op jit(solution)/shard_map/while/body/eval_jaxpr/gather | solution.py:59
  239.4 7.3 copy.43
  249.5 5.7 copy.44
  255.2 6.5 copy.62
  261.6 6.8 copy.45
  268.4 88.3 %scatter_custom_fusion.3 = f32[64,3072]{0,1:T(8,128)S(1)} fusion(s32[16000]{0:T(1024)} %copy-done.3, f32[16000,64]{1,0:T(8,128)} %copy.45, f32[]{:T(128)} %constant.22.clone.1), kind=kCustom, calls=%fused_computation.47 | custom fusion | flops 1024000 | bytes 786944 | tf_op jit(solution)/shard_map/while/body/eval_jaxpr/scatter-add | solution.py:63
  356.8 4.5 collective-permute-start.6
  365.2 5.5 scatter_custom_fusion.4
  371.7 5.3 scatter_custom_fusion.5
  381.7 5.1 collective-permute-start.8
  389.6 7.6 all-to-all-start
  397.4 33.1 %gather_fusion.8 = bf16[16000,64]{1,0:T(8,128)(2,1)} fusion(bf16[64,3072]{0,1:T(8,128)(2,1)S(1)} %pad_maximum_fusion.2, s32[16384]{0:T(1024)S(1)} %pad_clamp_fusion), kind=kCustom, calls=%fused_computation.8 | custom fusion | bytes 4160000 | tf_op jit(solution)/shard_map/while/body/eval_jaxpr/gather | solution.py:59
  430.4 8.0 copy.47
  438.4 4.2 multiply_bitcast_fusion
  442.6 5.7 copy.48
  448.3 6.4 copy.61
  454.7 6.8 copy.49
  461.5 88.3 %scatter_custom_fusion.6 = f32[64,3072]{0,1:T(8,128)S(1)} fusion(s32[16000]{0:T(1024)} %copy-done.3, f32[16000,64]{1,0:T(8,128)} %copy.49, f32[]{:T(128)} %constant.22.clone.1), kind=kCustom, calls=%fused_computation.45 | custom fusion | flops 1024000 | bytes 786944 | tf_op jit(solution)/shard_map/while/body/eval_jaxpr/scatter-add | solution.py:63
  550.6 4.4 collective-permute-start.10
  561.2 5.3 scatter_custom_fusion.7
  566.5 5.3 scatter_custom_fusion.8
  573.6 16.5 %all_to_all.24 = bf16[4,64,512]{2,1,0:T(8,128)(2,1)S(1)} all-to-all(bf16[4,64,512]{2,1,0:T(8,128)(2,1)S(1)} %copy.50), channel_id=1, replica_groups=mesh['cells'=64,'bands'=4] {'bands'}, dimensions={0} | all-to-all | bytes 524288 | tf_op jit(solution)/shard_map/all_to_all | solution.py:87
  592.7 274.2 %all-reduce.3.cloned.1.call-done = f32[1024,64]{1,0:T(8,128)} async-done(((f32[1024,64]{1,0:T(8,128)}), f32[1024,64]{1,0:T(8,128)}) %all-reduce.3.cloned.1.call-update) | async-done | bytes 262160
  (83 shorter events, 64.1 us)
Async XLA Ops:
  7.2 12.2 %copy-start.1 = (s32[125,128]{1,0:T(8,128)S(1)}, s32[125,128]{1,0:T(8,128)}, u32[]{:S(2)}) copy-start(s32[125,128]{1,0:T(8,128)} %param.12) | copy-start | bytes 192004
  7.2 12.4 %copy-start.10 = (f32[128]{0:T(128)S(1)}, f32[128]{0:T(128)}, u32[]{:S(2)}) copy-start(f32[128]{0:T(128)} %param.10) | copy-start | bytes 1540
  7.2 12.4 %copy-start.9 = (f32[2]{0:T(128)S(1)}, f32[2]{0:T(128)}, u32[]{:S(2)}) copy-start(f32[2]{0:T(128)} %param.15) | copy-start | bytes 28
  8.0 7.4 copy-start.4
  8.0 7.4 copy-start.5
  10.6 10.3 %collective-permute-start = (bf16[64,512]{0,1:T(8,128)(2,1)S(1)}, bf16[64,512]{0,1:T(8,128)(2,1)S(1)}, u32[]{:S(2)}, u32[]{:S(2)}) collective-permute-start(bf16[64,512]{0,1:T(8,128)(2,1)S(1)} %bitcast.120), channel_id=1, source_target_pairs={{0,4},{4,8},{8,12},{12,16},{16,20},{20,24},{24,28},{28,32},{32,36}... | collective-permute-start | bytes 196616 | tf_op jit(solution)/shard_map/ppermute | solution.py:16
  15.4 6.9 collective-permute-start.1
  19.6 64.9 %copy-start.3 = (s32[16000]{0:T(1024)}, s32[16000]{0:T(1024)S(1)}, u32[]{:S(2)}) copy-start(s32[16000]{0:T(1024)S(1)} %fusion.30) | copy-start | bytes 192004
  19.6 43.2 %copy-start.6 = (f32[128]{0:T(128)}, f32[128]{0:T(128)S(1)}, u32[]{:S(2)}) copy-start(f32[128]{0:T(128)S(1)} %compare_select_fusion.4) | copy-start | bytes 1540
  55.5 7.4 copy-start
  84.5 95.6 %copy-start.2 = (f32[2048]{0:T(1024)S(1)}, f32[2048]{0:T(1024)}, u32[]{:S(2)}) copy-start(f32[2048]{0:T(1024)} %param.11) | copy-start | bytes 24580
  173.6 8.6 collective-permute-start.2
  176.8 10.6 %collective-permute-start.3 = (f32[64,512]{0,1:T(8,128)}, f32[64,512]{0,1:T(8,128)S(1)}, u32[]{:S(2)}, u32[]{:S(2)}) collective-permute-start(f32[64,512]{0,1:T(8,128)} %get-tuple-element.70), channel_id=1, source_target_pairs={{4,0},{8,4},{12,8},{16,12},{20,16},{24,20},{28,24},{32,28},{36,32}... | collective-permute-start | bytes 393224 | tf_op jit(solution)/shard_map/ppermute | solution.py:19
  194.6 6.9 collective-permute-start.4
  198.3 7.9 collective-permute-start.5
  239.4 7.3 copy-start.7
  356.8 8.3 collective-permute-start.6
  361.3 10.4 %collective-permute-start.7 = (f32[64,512]{0,1:T(8,128)S(1)}, f32[64,512]{0,1:T(8,128)S(1)}, u32[]{:S(2)}, u32[]{:S(2)}) collective-permute-start(f32[64,512]{0,1:T(8,128)S(1)} %get-tuple-element.68), channel_id=1, source_target_pairs={{4,0},{8,4},{12,8},{16,12},{20,16},{24,20},{28,24},{32,28},{36,32}... | collective-permute-start | bytes 393224 | tf_op jit(solution)/shard_map/ppermute | solution.py:19
  381.7 15.5 %collective-permute-start.8 = (bf16[64,512]{0,1:T(8,128)(2,1)S(1)}, bf16[64,512]{0,1:T(8,128)(2,1)S(1)}, u32[]{:S(2)}, u32[]{:S(2)}) collective-permute-start(bf16[64,512]{0,1:T(8,128)(2,1)S(1)} %bitcast.123), channel_id=1, source_target_pairs={{0,4},{4,8},{8,12},{12,16},{16,20},{20,24},{24,28},{28,32},{32,36}... | collective-permute-start | bytes 196616 | tf_op jit(solution)/shard_map/ppermute | solution.py:16
  386.8 10.4 %collective-permute-start.9 = (bf16[64,512]{0,1:T(8,128)(2,1)S(1)}, bf16[64,512]{0,1:T(8,128)(2,1)S(1)}, u32[]{:S(2)}, u32[]{:S(2)}) collective-permute-start(bf16[64,512]{0,1:T(8,128)(2,1)S(1)} %bitcast.121), channel_id=1, source_target_pairs={{4,0},{8,4},{12,8},{16,12},{20,16},{24,20},{28,24},{32,28},{36,32}... | collective-permute-start | bytes 196616 | tf_op jit(solution)/shard_map/ppermute | solution.py:19
  389.6 183.9 %all-to-all-start = ((bf16[64,4,512]{2,0,1:T(8,128)(2,1)}), bf16[64,4,512]{2,0,1:T(8,128)(2,1)S(1)}, u32[]{:S(2)}, u32[]{:S(2)}) async-start(bf16[64,4,512]{2,0,1:T(8,128)(2,1)} %copy.46), calls=%async_computation | async-start | bytes 524288 | tf_op jit(solution)/shard_map/all_to_all | solution.py:96
  397.2 469.7 %all-reduce.3.cloned.1.call-start = ((), (), s32[]{:S(2)}) async-start(), calls=%async_computation.2 | async-start | bytes 1048576
  430.4 8.0 copy-start.8
  550.6 10.6 %collective-permute-start.10 = (f32[64,512]{0,1:T(8,128)S(1)}, f32[64,512]{0,1:T(8,128)S(1)}, u32[]{:S(2)}, u32[]{:S(2)}) collective-permute-start(f32[64,512]{0,1:T(8,128)S(1)} %get-tuple-element.67), channel_id=1, source_target_pairs={{0,4},{4,8},{8,12},{12,16},{16,20},{20,24},{24,28},{28,32},{32,36}... | collective-permute-start | bytes 393224 | tf_op jit(solution)/shard_map/ppermute | solution.py:16
  555.0 11.5 %collective-permute-start.11 = (f32[64,512]{0,1:T(8,128)}, f32[64,512]{0,1:T(8,128)S(1)}, u32[]{:S(2)}, u32[]{:S(2)}) collective-permute-start(f32[64,512]{0,1:T(8,128)} %get-tuple-element.66), channel_id=1, source_target_pairs={{4,0},{8,4},{12,8},{16,12},{20,16},{24,20},{28,24},{32,28},{36,32}... | collective-permute-start | bytes 393224 | tf_op jit(solution)/shard_map/ppermute | solution.py:19
Sparse Core Ops, SparseCore 0:
  591.7 275.1 all-reduce.2
